TPU v7x, 32 devices: a whole 2x2x4 slice. The times are simulated.
32 devices in a mesh: dp: 4 (over y, x), expert: 8 (over z, core).
Axes of the slice: x: 2, y: 2, z: 4, core: 2. Of those that a mesh axis runs over, the one named last changes fastest.
Arguments:
- tokens: bfloat16 [1024, 1024], P(('dp', 'expert')), may hold values from -6 to 6
- cotangent: bfloat16 [1024, 1024], P(('dp', 'expert')), may hold values from -3 to 3
- routes: int32 [1024, 8], P(('dp', 'expert')), may hold values from 0 to 7, as said below
- combine: bfloat16 [1024, 8], P(('dp', 'expert')), may hold values from 0.099609375 to 1
- hot_experts: int32 [4], replicated, may hold values from 0 to 3, as said below
- extra_slots: int32 [4], replicated, may hold values from 1 to 4, as said below
- w_gate: bfloat16 [8, 1024, 384], P('expert'), may hold values from -0.1875 to 0.1875
- w_up: bfloat16 [8, 1024, 384], P('expert'), may hold values from -0.1875 to 0.1875
- w_down: bfloat16 [8, 384, 1024], P('expert'), may hold values from -0.3125 to 0.3125
Outputs:
- token_grads: bfloat16 [1024, 1024], P(('dp', 'expert'))
- grad_gate: bfloat16 [8, 1024, 384], P('expert', 'dp')
- grad_up: bfloat16 [8, 1024, 384], P('expert', 'dp')
- grad_down: bfloat16 [8, 384, 1024], P('expert')
Inputs may be any that keep to these rules, and one draw needn't show every extreme that they name: `routes`: each row names 8 different experts. `hot_experts`: 4 different experts, all below 4. `extra_slots`: one of the entries equals 4.
All inputs are finite; a program needn't handle non-finite values.
Results may differ from a plain program's by a relative error of at most 0.0064.
Values may be sent and summed in bfloat16 or wider, within the bound.
A program may use at most 64 MiB of HBM per device.

v0:
```python
import jax
import jax.numpy as jnp
from jax import lax
from jax.sharding import PartitionSpec as P


def forward_rows(weight_gate, weight_up, weight_down, row_tokens, row_cotan, row_weights):
    gate_pre = jnp.dot(row_tokens, weight_gate, preferred_element_type=jnp.float32)
    up_proj = jnp.dot(row_tokens, weight_up, preferred_element_type=jnp.float32)
    sigmoid_gate = jax.nn.sigmoid(gate_pre)
    gate_act = gate_pre * sigmoid_gate
    hidden = (gate_act * up_proj).astype(jnp.bfloat16)
    out_grad = (row_weights.astype(jnp.float32)[:, None] * row_cotan.astype(jnp.float32)).astype(
        jnp.bfloat16
    )
    hidden_grad = jnp.dot(out_grad, weight_down.T, preferred_element_type=jnp.float32)
    gate_grad = (
        hidden_grad * up_proj * sigmoid_gate * (1.0 + gate_pre * (1.0 - sigmoid_gate))
    ).astype(jnp.bfloat16)
    up_grad = (hidden_grad * gate_act).astype(jnp.bfloat16)
    row_grads = jnp.dot(gate_grad, weight_gate.T, preferred_element_type=jnp.float32)
    row_grads = row_grads + jnp.dot(up_grad, weight_up.T, preferred_element_type=jnp.float32)
    return (row_grads.astype(jnp.bfloat16), (row_tokens, gate_grad, up_grad, hidden, out_grad))


def weight_terms(pieces):
    row_tokens, gate_grad, up_grad, hidden, out_grad = pieces
    grad_gate = jnp.dot(row_tokens.T, gate_grad, preferred_element_type=jnp.float32)
    grad_up = jnp.dot(row_tokens.T, up_grad, preferred_element_type=jnp.float32)
    grad_down = jnp.dot(hidden.T, out_grad, preferred_element_type=jnp.float32)
    return (grad_gate, grad_up, grad_down)


def expert_pass(weight_gate, weight_up, weight_down, row_tokens, row_cotan, row_weights):
    row_grads, pieces = forward_rows(
        weight_gate, weight_up, weight_down, row_tokens, row_cotan, row_weights
    )
    return (row_grads, weight_terms(pieces))


def shards(tokens, cotangent, routes, combine, hot_experts, extra_slots, w_gate, w_up, w_down):
    expert_count = lax.axis_size("expert")
    token_count, features = tokens.shape
    route_count = routes.shape[1]
    capacity = max(2, min(token_count * route_count * 7 // (8 * expert_count), token_count // 2))
    spare_slots = 2 * max(1, capacity // 6)
    expert_ids = routes.reshape(-1)
    assign_count = expert_ids.shape[0]
    assign_order = jnp.arange(assign_count, dtype=jnp.int32)
    earlier = (expert_ids[:, None] == expert_ids[None, :]) & (
        assign_order[None, :] < assign_order[:, None]
    )
    slot_rank = jnp.sum(earlier.astype(jnp.int32), axis=1)
    hot_match = expert_ids[:, None] == hot_experts[None, :]
    slot_limit = capacity + jnp.sum(jnp.where(hot_match, extra_slots[None, :], 0), axis=1)
    is_kept = slot_rank < slot_limit
    slot_count = capacity + spare_slots
    total_slots = expert_count * slot_count
    flat_slot = jnp.where(is_kept, expert_ids * slot_count + slot_rank, total_slots)
    slot_ids = jnp.arange(total_slots, dtype=jnp.int32)
    assign_onehot = slot_ids[:, None] == flat_slot[None, :]
    token_onehot = jnp.any(
        assign_onehot.reshape(total_slots, token_count, route_count), axis=2
    ).astype(jnp.bfloat16)
    both_rows = jnp.concatenate([tokens, cotangent], axis=1)
    filled = jnp.dot(token_onehot, both_rows, preferred_element_type=jnp.float32).astype(
        jnp.bfloat16
    )
    token_send = filled[:, :features].reshape(expert_count, slot_count, features)
    cotan_send = filled[:, features:].reshape(expert_count, slot_count, features)
    weight_flat = jnp.sum(
        jnp.where(assign_onehot, combine.reshape(-1).astype(jnp.float32)[None, :], 0.0), axis=1
    )
    weight_send = weight_flat.astype(jnp.bfloat16).reshape(expert_count, slot_count)
    token_recv, cotan_recv, weight_recv = (
        lax.all_to_all(token_send, "expert", split_axis=0, concat_axis=0, tiled=True),
        lax.all_to_all(cotan_send, "expert", split_axis=0, concat_axis=0, tiled=True),
        lax.all_to_all(weight_send, "expert", split_axis=0, concat_axis=0, tiled=True),
    )
    own_weights = (w_gate[0], w_up[0], w_down[0])
    all_rows, grad_terms = expert_pass(
        own_weights[0],
        own_weights[1],
        own_weights[2],
        token_recv.reshape(-1, features),
        cotan_recv.reshape(-1, features),
        weight_recv.reshape(-1),
    )
    grad_rows = all_rows.reshape(expert_count, slot_count, features)
    returned_rows = lax.all_to_all(grad_rows, "expert", split_axis=0, concat_axis=0, tiled=True)
    token_grads = jnp.dot(
        token_onehot.T,
        returned_rows.reshape(total_slots, features),
        preferred_element_type=jnp.float32,
    ).astype(jnp.bfloat16)
    grad_gate, grad_up = (
        lax.psum_scatter(grad_terms[0][None], "dp", scatter_dimension=1, tiled=True),
        lax.psum_scatter(grad_terms[1][None], "dp", scatter_dimension=1, tiled=True),
    )
    grad_down = lax.psum(grad_terms[2][None], "dp")
    return (
        token_grads,
        grad_gate.astype(jnp.bfloat16),
        grad_up.astype(jnp.bfloat16),
        grad_down.astype(jnp.bfloat16),
    )


def solution(mesh):
    in_specs = (
        P(("dp", "expert"), None),
        P(("dp", "expert"), None),
        P(("dp", "expert"), None),
        P(("dp", "expert"), None),
        P(),
        P(),
        P("expert", None, None),
        P("expert", None, None),
        P("expert", None, None),
    )
    out_specs = (
        P(("dp", "expert"), None),
        P("expert", "dp", None),
        P("expert", "dp", None),
        P("expert", None, None),
    )
    return jax.shard_map(shards, mesh=mesh, in_specs=in_specs, out_specs=out_specs, check_vma=False)
```

profile of v0, /device:TPU:0, one launch (start us, length us, event | category | flops | bytes accessed | tf_op | source)
XLA Modules:
  0.0 155.9 jit_solution(16793875699837294183)
XLA Ops:
  7.2 0.8 copy.24
  8.3 0.8 copy.26
  9.1 0.8 select_reduce_fusion.1
  10.0 0.7 convert_element_type.116
  10.7 6.4 %all-to-all-start = ((bf16[8,1,20]{2,1,0:T(2,128)(2,1)}), bf16[8,1,20]{2,1,0:T(2,128)(2,1)S(1)}, u32[]{:S(2)}, u32[]{:S(2)}) async-start(bf16[8,1,20]{2,1,0:T(2,128)(2,1)} %convert_element_type.116), calls=%async_computation | async-start | bytes 8192 | tf_op jit(solution)/shard_map/all_to_all | solution.py:78
  17.4 1.2 convolution_convert_fusion
  18.7 0.8 reshape.99
  19.5 3.0 %all-to-all-done = bf16[8,1,20]{2,1,0:T(2,128)(2,1)S(1)} async-done(((bf16[8,1,20]{2,1,0:T(2,128)(2,1)}), bf16[8,1,20]{2,1,0:T(2,128)(2,1)S(1)}, u32[]{:S(2)}, u32[]{:S(2)}) %all-to-all-start) | async-done | bytes 352 | tf_op jit(solution)/shard_map/all_to_all | solution.py:78
  22.6 3.5 %all-to-all-start.2 = ((bf16[8,20,1024]{2,1,0:T(8,128)(2,1)}), bf16[8,20,1024]{2,1,0:T(8,128)(2,1)S(1)}, u32[]{:S(2)}, u32[]{:S(2)}) async-start(bf16[8,20,1024]{2,1,0:T(8,128)(2,1)} %reshape.99), calls=%async_computation.2 | async-start | bytes 786432 | tf_op jit(solution)/shard_map/all_to_all | solution.py:76
  26.1 0.8 reshape.98
  26.9 11.6 %all-to-all-done.2 = bf16[8,20,1024]{2,1,0:T(8,128)(2,1)S(1)} async-done(((bf16[8,20,1024]{2,1,0:T(8,128)(2,1)}), bf16[8,20,1024]{2,1,0:T(8,128)(2,1)S(1)}, u32[]{:S(2)}, u32[]{:S(2)}) %all-to-all-start.2) | async-done | bytes 327712 | tf_op jit(solution)/shard_map/all_to_all | solution.py:76
  38.5 3.5 %all-to-all-start.1 = ((bf16[8,20,1024]{2,1,0:T(8,128)(2,1)}), bf16[8,20,1024]{2,1,0:T(8,128)(2,1)S(1)}, u32[]{:S(2)}, u32[]{:S(2)}) async-start(bf16[8,20,1024]{2,1,0:T(8,128)(2,1)} %reshape.98), calls=%async_computation.1 | async-start | bytes 786432 | tf_op jit(solution)/shard_map/all_to_all | solution.py:77
  42.8 11.6 %all-to-all-done.1 = bf16[8,20,1024]{2,1,0:T(8,128)(2,1)S(1)} async-done(((bf16[8,20,1024]{2,1,0:T(8,128)(2,1)}), bf16[8,20,1024]{2,1,0:T(8,128)(2,1)S(1)}, u32[]{:S(2)}, u32[]{:S(2)}) %all-to-all-start.1) | async-done | bytes 327712 | tf_op jit(solution)/shard_map/all_to_all | solution.py:77
  54.6 1.6 multiply_convert_fusion.4
  56.2 1.6 %convolution_bitcast_fusion.2 = f32[1,1024,384]{2,1,0:T(8,128)} fusion(bf16[160,1024]{1,0:T(8,128)(2,1)S(1)} %reshape.100, bf16[160,384]{1,0:T(8,128)(2,1)S(1)} %get-tuple-element.7), kind=kOutput, calls=%fused_computation.3 | convolution fusion | flops 125829120 | bytes 2023424 | tf_op jit(solution)/shard_map/dot_general | solution.py:28
  57.9 1.6 %convolution_bitcast_fusion.1 = f32[1,1024,384]{2,1,0:T(8,128)} fusion(bf16[160,1024]{1,0:T(8,128)(2,1)S(1)} %reshape.100, bf16[160,384]{1,0:T(8,128)(2,1)S(1)} %get-tuple-element.6), kind=kOutput, calls=%fused_computation.2 | convolution fusion | flops 125829120 | bytes 2023424 | tf_op jit(solution)/shard_map/dot_general | solution.py:29
  59.6 0.4 fusion.1
  60.5 0.8 reshape.101
  61.3 3.5 %all-to-all-start.3 = ((bf16[8,20,1024]{2,1,0:T(8,128)(2,1)}), bf16[8,20,1024]{2,1,0:T(8,128)(2,1)S(1)}, u32[]{:S(2)}, u32[]{:S(2)}) async-start(bf16[8,20,1024]{2,1,0:T(8,128)(2,1)} %reshape.101), calls=%async_computation.3 | async-start | bytes 786432 | tf_op jit(solution)/shard_map/all_to_all | solution.py:90
  64.8 1.5 convolution_bitcast_fusion
  66.3 78.5 %all-reduce.1 = bf16[1,384,1024]{2,1,0:T(8,128)(2,1)} all-reduce(f32[1,384,1024]{2,1,0:T(8,128)S(1)} %convolution_bitcast_fusion), channel_id=1, replica_groups=mesh['dp'=4,'expert'=8] {'dp'}, use_global_device_ids=true, to_apply=%region_6.7 | all-reduce | flops 393216 | bytes 2359296 | tf_op jit(solution)/shard_map/psum | solution.py:100
  144.9 0.8 convolution_convert_fusion.1
  145.7 1.7 %convert_element_type.103 = bf16[1,256,384]{2,1,0:T(8,128)(2,1)} convert(f32[1,256,384]{2,1,0:T(8,128)} %reduce-scatter.3.cloned.1.call-done) | non-fusion elementwise | flops 98304 | bytes 589824 | tf_op jit(solution)/shard_map/convert_element_type | solution.py:103
  147.4 1.7 %convert_element_type.104 = bf16[1,256,384]{2,1,0:T(8,128)(2,1)} convert(f32[1,256,384]{2,1,0:T(8,128)} %reduce-scatter.5.cloned.1.call-done) | non-fusion elementwise | flops 98304 | bytes 589824 | tf_op jit(solution)/shard_map/convert_element_type | solution.py:104
  (36 shorter events, 2.6 us)
Async XLA Ops:
  7.2 34.9 %copy-start = (bf16[1,1024,384]{2,1,0:T(8,128)(2,1)S(1)}, bf16[1,1024,384]{2,1,0:T(8,128)(2,1)}, u32[]{:S(2)}) copy-start(bf16[1,1024,384]{2,1,0:T(8,128)(2,1)} %param.15) | copy-start | bytes 2359300
  10.7 11.9 %all-to-all-start = ((bf16[8,1,20]{2,1,0:T(2,128)(2,1)}), bf16[8,1,20]{2,1,0:T(2,128)(2,1)S(1)}, u32[]{:S(2)}, u32[]{:S(2)}) async-start(bf16[8,1,20]{2,1,0:T(2,128)(2,1)} %convert_element_type.116), calls=%async_computation | async-start | bytes 8192 | tf_op jit(solution)/shard_map/all_to_all | solution.py:78
  22.6 15.9 %all-to-all-start.2 = ((bf16[8,20,1024]{2,1,0:T(8,128)(2,1)}), bf16[8,20,1024]{2,1,0:T(8,128)(2,1)S(1)}, u32[]{:S(2)}, u32[]{:S(2)}) async-start(bf16[8,20,1024]{2,1,0:T(8,128)(2,1)} %reshape.99), calls=%async_computation.2 | async-start | bytes 786432 | tf_op jit(solution)/shard_map/all_to_all | solution.py:76
  26.9 15.6 %copy-start.1 = (bf16[1,1024,384]{2,1,0:T(8,128)(2,1)S(1)}, bf16[1,1024,384]{2,1,0:T(8,128)(2,1)}, u32[]{:S(2)}) copy-start(bf16[1,1024,384]{2,1,0:T(8,128)(2,1)} %param.16) | copy-start | bytes 2359300
  38.5 15.9 %all-to-all-start.1 = ((bf16[8,20,1024]{2,1,0:T(8,128)(2,1)}), bf16[8,20,1024]{2,1,0:T(8,128)(2,1)S(1)}, u32[]{:S(2)}, u32[]{:S(2)}) async-start(bf16[8,20,1024]{2,1,0:T(8,128)(2,1)} %reshape.98), calls=%async_computation.1 | async-start | bytes 786432 | tf_op jit(solution)/shard_map/all_to_all | solution.py:77
  42.0 103.7 %reduce-scatter.3.cloned.1.call-start = ((), (), s32[]{:S(2)}) async-start(), calls=%async_computation.6 | async-start | bytes 1966080 | tf_op jit(solution)/shard_map/reduce_scatter | solution.py:97
  42.5 17.1 %copy-start.2 = (f32[160,384]{1,0:T(8,128)}, f32[160,384]{1,0:T(8,128)S(1)}, u32[]{:S(2)}) copy-start(f32[160,384]{1,0:T(8,128)S(1)} %fusion.3) | copy-start | bytes 737284
  42.8 16.7 %copy-start.3 = (f32[160,384]{1,0:T(8,128)}, f32[160,384]{1,0:T(8,128)S(1)}, u32[]{:S(2)}) copy-start(f32[160,384]{1,0:T(8,128)S(1)} %fusion.6) | copy-start | bytes 737284
  57.8 89.6 %reduce-scatter.5.cloned.1.call-start = ((), (), s32[]{:S(2)}) async-start(), calls=%async_computation.7 | async-start | bytes 1966080 | tf_op jit(solution)/shard_map/reduce_scatter | solution.py:98
  61.3 83.5 %all-to-all-start.3 = ((bf16[8,20,1024]{2,1,0:T(8,128)(2,1)}), bf16[8,20,1024]{2,1,0:T(8,128)(2,1)S(1)}, u32[]{:S(2)}, u32[]{:S(2)}) async-start(bf16[8,20,1024]{2,1,0:T(8,128)(2,1)} %reshape.101), calls=%async_computation.3 | async-start | bytes 786432 | tf_op jit(solution)/shard_map/all_to_all | solution.py:90
Sparse Core Ops, SparseCore 0:
  57.9 36.4 reduce-scatter.2
  97.4 43.6 reduce-scatter.4
where the time goes:
time: 157 us; the launch traced here: 156 us
  blocking collectives  78.5 us (50%)
  waiting for transfers between devices  26.3 us (17%)
  starting transfers between devices  16.8 us (11%)
  between operations  14.2 us (9%)
  matrix products  9.84 us (6%)
  local copies, waits for them, and re-layouts  5.47 us (3%)
  other arithmetic  4.81 us (3%)
    psum x1, blocking collectives, shards(): grad_down = lax.psum(grad_terms[2][None], 'dp')  78.5 us
    all_to_all x1, waiting for transfers between devices, shards(): lax.all_to_all(token_send, 'expert', split_axis=0, concat_axis=0, tiled=T...  11.6 us
    all_to_all x1, waiting for transfers between devices, shards(): lax.all_to_all(cotan_send, 'expert', split_axis=0, concat_axis=0, tiled=T...  11.6 us
    all_to_all x1, starting transfers between devices, shards(): lax.all_to_all(weight_send, 'expert', split_axis=0, concat_axis=0, tiled=...  6.35 us
    all_to_all x1, starting transfers between devices, shards(): lax.all_to_all(grad_rows, 'expert', split_axis=0, concat_axis=0, tiled=True)  3.46 us
    all_to_all x1, starting transfers between devices, shards(): lax.all_to_all(token_send, 'expert', split_axis=0, concat_axis=0, tiled=T...  3.45 us
    all_to_all x1, starting transfers between devices, shards(): lax.all_to_all(cotan_send, 'expert', split_axis=0, concat_axis=0, tiled=T...  3.45 us
  transfers between devices with their start and end apart: 6, of which 3 were waited for; matrix products, arithmetic and copies ran while one was open for 7% of the time, Pallas kernels for 0%

commit v1 on v0

--- a/solution.py
+++ b/solution.py
@@ -97,7 +97,7 @@
         lax.psum_scatter(grad_terms[0][None], "dp", scatter_dimension=1, tiled=True),
         lax.psum_scatter(grad_terms[1][None], "dp", scatter_dimension=1, tiled=True),
     )
-    grad_down = lax.psum(grad_terms[2][None], "dp")
+    grad_down = jnp.sum(lax.all_gather(grad_terms[2][None], "dp"), axis=0)
     return (
         token_grads,
         grad_gate.astype(jnp.bfloat16),

time: 157 us -> 206 us (1.31)
  waiting for transfers between devices: 26.3 us -> 138 us
  blocking collectives: 78.5 us -> 14.9 us
  other arithmetic: 4.81 us -> 9.38 us
  starting transfers between devices: 16.8 us -> 13.4 us
    psum x1 -> x0, blocking collectives: 78.5 us -> none  [shards(): grad_down = lax.psum(grad_terms[2][None], 'dp')]
    all_gather x0 -> x1, waiting for transfers between devices: none -> 70.2 us  [shards(): grad_down = jnp.sum(lax.all_gather(grad_terms[2][None], 'dp'), axis=0)]
    reduce_scatter x1, waiting for transfers between devices: 0.01 us -> 32.4 us  [shards(): lax.psum_scatter(grad_terms[1][None], 'dp', scatter_dimension=1, tiled=True)]
    all_to_all x0 -> x1, blocking collectives: none -> 14.9 us  [shards(): lax.all_to_all(grad_rows, 'expert', split_axis=0, concat_axis=0, tiled=True)]
    reduce_scatter x1, waiting for transfers between devices: 0.01 us -> 9.4 us  [shards(): lax.psum_scatter(grad_terms[0][None], 'dp', scatter_dimension=1, tiled=True)]
    reduce_sum x0 -> x1, other arithmetic: none -> 4.58 us  [shards(): grad_down = jnp.sum(lax.all_gather(grad_terms[2][None], 'dp'), axis=0)]
    all_to_all x1 -> x0, starting transfers between devices: 3.46 us -> none  [shards(): lax.all_to_all(grad_rows, 'expert', split_axis=0, concat_axis=0, tiled=True)]
  transfers between devices with their start and end apart: 6 -> 6, of which waited for: 3 -> 6; matrix products, arithmetic and copies ran while one was open for 7% -> 6% of each run, Pallas kernels for 0% -> 0%
where the time goes in v1:
time: 206 us; the launch traced here: 205 us
  waiting for transfers between devices  138 us (67%)
  blocking collectives  14.9 us (7%)
  between operations  14 us (7%)
  starting transfers between devices  13.4 us (7%)
  matrix products  10 us (5%)
  other arithmetic  9.38 us (5%)
  local copies, waits for them, and re-layouts  5.19 us (3%)
    all_gather x1, waiting for transfers between devices, shards(): grad_down = jnp.sum(lax.all_gather(grad_terms[2][None], 'dp'), axis=0)  70.2 us
    reduce_scatter x1, waiting for transfers between devices, shards(): lax.psum_scatter(grad_terms[1][None], 'dp', scatter_dimension=1, tiled=True)  32.4 us
    all_to_all x1, blocking collectives, shards(): lax.all_to_all(grad_rows, 'expert', split_axis=0, concat_axis=0, tiled=True)  14.9 us
    all_to_all x1, waiting for transfers between devices, shards(): lax.all_to_all(token_send, 'expert', split_axis=0, concat_axis=0, tiled=T...  11.6 us
    all_to_all x1, waiting for transfers between devices, shards(): lax.all_to_all(cotan_send, 'expert', split_axis=0, concat_axis=0, tiled=T...  11.6 us
    reduce_scatter x1, waiting for transfers between devices, shards(): lax.psum_scatter(grad_terms[0][None], 'dp', scatter_dimension=1, tiled=True)  9.4 us
    all_to_all x1, starting transfers between devices, shards(): lax.all_to_all(weight_send, 'expert', split_axis=0, concat_axis=0, tiled=...  6.35 us
    reduce_sum x1, other arithmetic, shards(): grad_down = jnp.sum(lax.all_gather(grad_terms[2][None], 'dp'), axis=0)  4.58 us
  transfers between devices with their start and end apart: 6, of which 6 were waited for; matrix products, arithmetic and copies ran while one was open for 6% of the time, Pallas kernels for 0%

profile of v1, /device:TPU:0, one launch (start us, length us, event | category | flops | bytes accessed | tf_op | source)
XLA Modules:
  0.0 205.2 jit_solution(9614905542292562590)
XLA Ops:
  7.2 0.8 copy.24
  8.3 0.8 copy.26
  9.1 0.8 select_reduce_fusion.1
  10.7 6.4 %all-to-all-start = ((bf16[8,1,20]{2,1,0:T(2,128)(2,1)}), bf16[8,1,20]{2,1,0:T(2,128)(2,1)S(1)}, u32[]{:S(2)}, u32[]{:S(2)}) async-start(bf16[8,1,20]{2,1,0:T(2,128)(2,1)} %convert_element_type.128), calls=%async_computation | async-start | bytes 8192 | tf_op jit(solution)/shard_map/all_to_all | solution.py:78
  17.4 1.2 convolution_convert_fusion
  18.7 0.8 reshape.109
  19.5 3.0 %all-to-all-done = bf16[8,1,20]{2,1,0:T(2,128)(2,1)S(1)} async-done(((bf16[8,1,20]{2,1,0:T(2,128)(2,1)}), bf16[8,1,20]{2,1,0:T(2,128)(2,1)S(1)}, u32[]{:S(2)}, u32[]{:S(2)}) %all-to-all-start) | async-done | bytes 352 | tf_op jit(solution)/shard_map/all_to_all | solution.py:78
  22.6 3.5 %all-to-all-start.2 = ((bf16[8,20,1024]{2,1,0:T(8,128)(2,1)}), bf16[8,20,1024]{2,1,0:T(8,128)(2,1)S(1)}, u32[]{:S(2)}, u32[]{:S(2)}) async-start(bf16[8,20,1024]{2,1,0:T(8,128)(2,1)} %reshape.109), calls=%async_computation.2 | async-start | bytes 786432 | tf_op jit(solution)/shard_map/all_to_all | solution.py:76
  26.1 0.8 reshape.108
  26.9 11.6 %all-to-all-done.2 = bf16[8,20,1024]{2,1,0:T(8,128)(2,1)S(1)} async-done(((bf16[8,20,1024]{2,1,0:T(8,128)(2,1)}), bf16[8,20,1024]{2,1,0:T(8,128)(2,1)S(1)}, u32[]{:S(2)}, u32[]{:S(2)}) %all-to-all-start.2) | async-done | bytes 327712 | tf_op jit(solution)/shard_map/all_to_all | solution.py:76
  38.5 3.5 %all-to-all-start.1 = ((bf16[8,20,1024]{2,1,0:T(8,128)(2,1)}), bf16[8,20,1024]{2,1,0:T(8,128)(2,1)S(1)}, u32[]{:S(2)}, u32[]{:S(2)}) async-start(bf16[8,20,1024]{2,1,0:T(8,128)(2,1)} %reshape.108), calls=%async_computation.1 | async-start | bytes 786432 | tf_op jit(solution)/shard_map/all_to_all | solution.py:77
  42.8 11.6 %all-to-all-done.1 = bf16[8,20,1024]{2,1,0:T(8,128)(2,1)S(1)} async-done(((bf16[8,20,1024]{2,1,0:T(8,128)(2,1)}), bf16[8,20,1024]{2,1,0:T(8,128)(2,1)S(1)}, u32[]{:S(2)}, u32[]{:S(2)}) %all-to-all-start.1) | async-done | bytes 327712 | tf_op jit(solution)/shard_map/all_to_all | solution.py:77
  54.6 1.6 multiply_convert_fusion.4
  56.2 1.6 convolution_bitcast_fusion.1
  57.9 1.7 convolution_bitcast_fusion
  59.9 1.6 fusion.10
  62.9 14.9 %all_to_all.21 = bf16[8,20,1024]{2,1,0:T(8,128)(2,1)S(1)} all-to-all(bf16[8,20,1024]{2,1,0:T(8,128)(2,1)S(1)} %reshape.111), channel_id=1, replica_groups=mesh['dp'=4,'expert'=8] {'expert'}, dimensions={0} | all-to-all | bytes 655360 | tf_op jit(solution)/shard_map/all_to_all | solution.py:90
  77.9 0.8 convolution_convert_fusion.1
  78.7 9.4 %reduce-scatter.3.cloned.1.call-done = f32[1,256,384]{2,1,0:T(8,128)} async-done(((f32[1,1024,384]{2,1,0:T(8,128)}), f32[1,256,384]{2,1,0:T(8,128)}) %reduce-scatter.3.cloned.1.call-update) | async-done | bytes 393232 | tf_op jit(solution)/shard_map/reduce_scatter | solution.py:97
  88.1 1.7 convert_element_type.114
  89.8 32.4 %reduce-scatter.5.cloned.1.call-done = f32[1,256,384]{2,1,0:T(8,128)} async-done(((f32[1,1024,384]{2,1,0:T(8,128)}), f32[1,256,384]{2,1,0:T(8,128)}) %reduce-scatter.5.cloned.1.call-update) | async-done | bytes 393232 | tf_op jit(solution)/shard_map/reduce_scatter | solution.py:98
  122.2 1.7 convert_element_type.115
  123.9 70.2 %all-gather.3.cloned.1.call-done = f32[1536,1024]{1,0:T(8,128)} async-done(((f32[384,1024]{1,0:T(8,128)}), f32[1536,1024]{1,0:T(8,128)}) %all-gather.3.cloned.1.call-update) | async-done | bytes 6291472 | tf_op jit(solution)/shard_map/all_gather | solution.py:100
  194.1 4.6 %reduce.1 = bf16[384,1024]{1,0:T(8,128)(2,1)} reduce(f32[4,384,1024]{2,1,0:T(8,128)} %bitcast.36, f32[]{:T(128)} %constant.5.clone.1), dimensions={0}, to_apply=%region_6.7 | reduce | flops 1179648 | bytes 7077892 | tf_op jit(solution)/shard_map/reduce_sum | solution.py:100
  (42 shorter events, 4.3 us)
Async XLA Ops:
  7.2 34.9 %copy-start = (bf16[1,1024,384]{2,1,0:T(8,128)(2,1)S(1)}, bf16[1,1024,384]{2,1,0:T(8,128)(2,1)}, u32[]{:S(2)}) copy-start(bf16[1,1024,384]{2,1,0:T(8,128)(2,1)} %param.15) | copy-start | bytes 2359300
  10.7 11.9 %all-to-all-start = ((bf16[8,1,20]{2,1,0:T(2,128)(2,1)}), bf16[8,1,20]{2,1,0:T(2,128)(2,1)S(1)}, u32[]{:S(2)}, u32[]{:S(2)}) async-start(bf16[8,1,20]{2,1,0:T(2,128)(2,1)} %convert_element_type.128), calls=%async_computation | async-start | bytes 8192 | tf_op jit(solution)/shard_map/all_to_all | solution.py:78
  22.6 15.9 %all-to-all-start.2 = ((bf16[8,20,1024]{2,1,0:T(8,128)(2,1)}), bf16[8,20,1024]{2,1,0:T(8,128)(2,1)S(1)}, u32[]{:S(2)}, u32[]{:S(2)}) async-start(bf16[8,20,1024]{2,1,0:T(8,128)(2,1)} %reshape.109), calls=%async_computation.2 | async-start | bytes 786432 | tf_op jit(solution)/shard_map/all_to_all | solution.py:76
  26.9 15.6 %copy-start.1 = (bf16[1,1024,384]{2,1,0:T(8,128)(2,1)S(1)}, bf16[1,1024,384]{2,1,0:T(8,128)(2,1)}, u32[]{:S(2)}) copy-start(bf16[1,1024,384]{2,1,0:T(8,128)(2,1)} %param.16) | copy-start | bytes 2359300
  38.5 15.9 %all-to-all-start.1 = ((bf16[8,20,1024]{2,1,0:T(8,128)(2,1)}), bf16[8,20,1024]{2,1,0:T(8,128)(2,1)S(1)}, u32[]{:S(2)}, u32[]{:S(2)}) async-start(bf16[8,20,1024]{2,1,0:T(8,128)(2,1)} %reshape.108), calls=%async_computation.1 | async-start | bytes 786432 | tf_op jit(solution)/shard_map/all_to_all | solution.py:77
  42.0 46.1 %reduce-scatter.3.cloned.1.call-start = ((), (), s32[]{:S(2)}) async-start(), calls=%async_computation.6 | async-start | bytes 1966080 | tf_op jit(solution)/shard_map/reduce_scatter | solution.py:97
  56.2 1.7 copy-start.2
  56.2 1.7 copy-start.4
  57.9 64.3 %reduce-scatter.5.cloned.1.call-start = ((), (), s32[]{:S(2)}) async-start(), calls=%async_computation.7 | async-start | bytes 1966080 | tf_op jit(solution)/shard_map/reduce_scatter | solution.py:98
  59.6 134.4 %all-gather.3.cloned.1.call-start = ((), (), s32[]{:S(2)}) async-start(), calls=%async_computation.8 | async-start | bytes 7864320 | tf_op jit(solution)/shard_map/all_gather | solution.py:100
  59.9 1.7 copy-start.3
  61.5 0.9 copy-start.5
Sparse Core Ops, SparseCore 0:
  58.0 30.0 reduce-scatter.2
  91.0 31.0 reduce-scatter.4
  124.0 69.9 all-gather.2
